TPU v7x, 32 devices: a whole 2x2x4 slice. The times are simulated.
32 devices in a mesh: wide: 16 (over z, y, core), shift: 2 (over x).
Axes of the slice: x: 2, y: 2, z: 4, core: 2. Of those that a mesh axis runs over, the one named last changes fastest.
Arguments:
- particles: bfloat16 [1024, 8448], P('wide'), may hold values from -64 to 64
- group_id: int32 [1024, 1], P('wide'), may hold values from 0 to 15; in each aligned block of 64 rows (0 to 63, 64 to 127, ...) at most 8 rows name the same one
- ctf_curves: float32 [16, 4224], P('wide'), may hold values from -1 to 1
- projections: bfloat16 [16, 8448], P('wide')
- inv_noise: float32 [4224], replicated, may hold values from 0.5 to 2
- shifts: int32 [64, 2], P('shift'), may hold values from -8 to 8
Outputs:
- insertion: float32 [16, 12672], P('wide')
- log_evidence: float32 [1024], P('wide')
Inputs may be any that keep to these rules, and one draw needn't show every extreme that they name: `group_id`: at most 8 of the rows of one device name the same group, a bound that some block reaches.
All inputs are finite; a program needn't handle non-finite values.
Results may differ from a plain program's by a relative error of at most 0.0029.
Values may be sent and summed in bfloat16 or wider, within the bound.
A program may use at most 64 MiB of HBM per device.

v0:
```python
import math
import jax
import jax.numpy as jnp
from jax import lax
from jax.sharding import PartitionSpec as P

TWO_PI_BOX = 2.0 * math.pi / 128.0
HIGHEST_PRECISION = lax.Precision.HIGHEST


def shift_tables(shifts, coeffs):
    coeff_index = jnp.arange(coeffs, dtype=jnp.int32)
    freq_x = (coeff_index // 128).astype(jnp.float32)
    freq_y = (coeff_index % 128 - 64).astype(jnp.float32)
    move_x = shifts[:, 0].astype(jnp.float32)
    move_y = shifts[:, 1].astype(jnp.float32)
    phase_angle = TWO_PI_BOX * (
        move_x[:, None] * freq_x[None, :] + move_y[:, None] * freq_y[None, :]
    )
    return (jnp.cos(phase_angle), jnp.sin(phase_angle))


def rotate_slices(slab, cos_table, sin_table):
    coeffs = cos_table.shape[1]
    real_part = slab[:, :coeffs].astype(jnp.float32)[:, None, :]
    imag_part = slab[:, coeffs:].astype(jnp.float32)[:, None, :]
    rot_real = real_part * cos_table[None] + imag_part * sin_table[None]
    rot_imag = imag_part * cos_table[None] - real_part * sin_table[None]
    joined = jnp.concatenate([rot_real, rot_imag], 2)
    return joined.reshape(slab.shape[0] * cos_table.shape[0], 2 * coeffs).astype(jnp.bfloat16)


def slice_scores(weighted, weight_sq, slab, cos_table, sin_table):
    coeffs = cos_table.shape[1]
    n_trans = cos_table.shape[0]
    row_count = weighted.shape[0]
    rotated = rotate_slices(slab, cos_table, sin_table)
    cross_term = lax.dot_general(
        weighted, rotated, (((1,), (1,)), ((), ())), preferred_element_type=jnp.float32
    )
    slice_real = slab[:, :coeffs].astype(jnp.float32)
    slice_imag = slab[:, coeffs:].astype(jnp.float32)
    slice_power = slice_real * slice_real + slice_imag * slice_imag
    self_term = 0.5 * lax.dot_general(
        weight_sq, slice_power, (((1,), (1,)), ((), ())), precision=HIGHEST_PRECISION
    )
    scores = cross_term.reshape(row_count, slab.shape[0], n_trans) - self_term[:, :, None]
    return scores.reshape(row_count, slab.shape[0] * n_trans)


def local(particles, group_id, ctf_curves, projections, inv_noise, shifts):
    coeffs = inv_noise.shape[0]
    n_trans = shifts.shape[0]
    part_rows = particles.shape[0]
    cos_table, sin_table = shift_tables(shifts, coeffs)
    groups = group_id[:, 0]
    gathered_ctf = lax.all_gather(ctf_curves, "wide", axis=0, tiled=True)
    choose_group = (
        groups[:, None] == jnp.arange(gathered_ctf.shape[0], dtype=jnp.int32)[None, :]
    ).astype(jnp.float32)
    ctf_row = jnp.dot(choose_group, gathered_ctf, precision=HIGHEST_PRECISION)
    live_rows = jnp.ones((part_rows,), jnp.float32)
    row_count = particles.shape[0]
    real_part = particles[:, :coeffs].astype(jnp.float32)
    imag_part = particles[:, coeffs:].astype(jnp.float32)
    noise_ctf = inv_noise[None, :] * ctf_row
    weighted = jnp.concatenate([noise_ctf * real_part, noise_ctf * imag_part], 1).astype(
        jnp.bfloat16
    )
    filtered = jnp.concatenate([ctf_row * real_part, ctf_row * imag_part], 1).astype(jnp.bfloat16)
    weight_sq = ctf_row * ctf_row * inv_noise[None, :]
    ctf_square = ctf_row * ctf_row
    slab = lax.all_gather(projections, "wide", axis=0, tiled=True)
    amount = slab.shape[0]
    block_len = math.gcd(amount, 16)
    blocks = slab.reshape(amount // block_len, block_len, slab.shape[1])
    results = lax.map(
        lambda slab_block: slice_scores(weighted, weight_sq, slab_block, cos_table, sin_table),
        blocks,
    )
    scores = jnp.moveaxis(results, 0, 1).reshape(row_count, amount * n_trans)
    local_max = jnp.max(scores, 1)
    row_max = lax.pmax(local_max, "shift")
    row_total = lax.psum(jnp.sum(jnp.exp(scores - row_max[:, None]), 1), "shift")
    weights = (jnp.exp(scores - row_max[:, None]) / row_total[:, None]).astype(jnp.bfloat16)
    log_evidence = row_max + jnp.log(row_total)
    amount = projections.shape[0] * lax.axis_size("wide")
    block_len = math.gcd(amount, 16)

    def one_block(block_id):
        first_orient = block_id * block_len
        weight_block = lax.dynamic_slice_in_dim(
            weights, first_orient * n_trans, block_len * n_trans, 1
        )
        update = lax.dot_general(
            weight_block, filtered, (((0,), (0,)), ((), ())), preferred_element_type=jnp.float32
        )
        update = update.reshape(block_len, n_trans, 2 * coeffs)
        upd_real = update[:, :, :coeffs]
        upd_imag = update[:, :, coeffs:]
        data_real = jnp.sum(upd_real * cos_table[None] - upd_imag * sin_table[None], 1)
        data_imag = jnp.sum(upd_real * sin_table[None] + upd_imag * cos_table[None], 1)
        weight_sum = (
            jnp.sum(weight_block.astype(jnp.float32).reshape(row_count, block_len, n_trans), 2)
            * live_rows[:, None]
        )
        weight_data = lax.dot_general(
            weight_sum, ctf_square, (((0,), (0,)), ((), ())), precision=HIGHEST_PRECISION
        )
        return jnp.concatenate([data_real, data_imag, weight_data], 1)

    results = lax.map(one_block, jnp.arange(amount // block_len, dtype=jnp.int32))
    summed = lax.psum_scatter(
        results.reshape(amount, 3 * coeffs), "wide", scatter_dimension=0, tiled=True
    )
    insertion = lax.psum(summed, "shift")
    return (insertion, log_evidence)


def solution(mesh):
    placed = (
        P("wide", None),
        P("wide", None),
        P("wide", None),
        P("wide", None),
        P(),
        P("shift", None),
    )
    return jax.shard_map(
        local, mesh=mesh, in_specs=placed, out_specs=(P("wide", None), P("wide")), check_vma=False
    )
```

profile of v0, /device:TPU:0, one launch (start us, length us, event | category | flops | bytes accessed | tf_op | source)
XLA Modules:
  0.0 188.0 jit_solution(715756407361464335)
XLA Ops:
  7.2 0.0 copy-start
  7.2 0.0 all-reduce.3.cloned.1.call-start
  7.2 0.8 convert_bitcast_fusion.1
  8.0 24.1 %all-gather = f32[16,1,4224]{2,1,0:T(1,128)S(1)} all-gather(f32[1,1,4224]{2,1,0:T(1,128)} %bitcast.41), channel_id=1, replica_groups=mesh['wide'=16,'shift'=2] {'wide'}, dimensions={0}, use_global_device_ids=true | all-gather | bytes 287232 | tf_op jit(solution)/shard_map/all_gather | solution.py:57
  32.1 19.1 %all-gather.1 = bf16[16,1,8448]{2,1,0:T(2,128)(2,1)S(1)} all-gather(bf16[1,1,8448]{2,1,0:T(2,128)(2,1)} %bitcast.40), channel_id=1, replica_groups=mesh['wide'=16,'shift'=2] {'wide'}, dimensions={0}, use_global_device_ids=true | all-gather | bytes 287232 | tf_op jit(solution)/shard_map/all_gather | solution.py:73
  51.3 2.1 %fusion.8 = (bf16[64,4224]{1,0:T(8,128)(2,1)S(1)}, bf16[64,4224]{1,0:T(8,128)(2,1)S(1)}, bf16[64,4224]{1,0:T(8,128)(2,1)S(1)}, bf16[64,4224]{1,0:T(8,128)(2,1)S(1)}, f32[64,4224]{1,0:T(8,128)S(1)}) fusion(bf16[64,8448]{1,0:T(8,128)(2,1)} %param.6, f32[4224]{0:T(1024)} %param.10, f32[16,1,4224]{2,1,0:T(1,128)S(1)} %all-gather, s32[64]{0:T(128)} %bitcast.42), kind=kOutput, calls=%fused_computation.15 | convolution fusion | flops 54879232 | bytes 4612864 | tf_op jit(solution)/shard_map/dot_general | solution.py:61
  53.5 0.0 copy-done
  53.5 1.1 convolution_multiply_fusion
  54.6 2.0 %fusion.21 = (f32[32,4224]{1,0:T(8,128)S(1)}, f32[32,4224]{1,0:T(8,128)S(1)}) fusion(f32[4224]{0:T(1024)S(1)} %get-tuple-element.64, f32[32]{0:T(128)S(1)} %get-tuple-element.59, f32[4224]{0:T(1024)S(1)} %get-tuple-element.63, f32[32]{0:T(128)S(1)} %get-tuple-element.58), kind=kLoop, calls=%fused_computation.32 | loop fusion | flops 540672 | bytes 1115392 | tf_op jit(solution)/shard_map/cos | solution.py:20
  56.6 2.2 %add_convert_fusion = (bf16[16,32,4224]{2,1,0:T(8,128)(2,1)S(1)}, bf16[16,32,4224]{2,1,0:T(8,128)(2,1)S(1)}) fusion(f32[32,4224]{1,0:T(8,128)S(1)} %get-tuple-element.57, f32[16,4224]{1,0:T(8,128)S(1)} %get-tuple-element.48, f32[32,4224]{1,0:T(8,128)S(1)} %get-tuple-element.56, f32[16,4224]{1,0:T(8,128)S(1)} %get-tuple-element.47), kind=kLoop, calls=%fused_computation.7 | loop fusion | flops 17301504 | bytes 10272768 | tf_op jit(solution)/shard_map/convert.2
  58.7 2.4 %fusion.46 = (f32[64]{0:T(128)S(1)}, f32[64,16,32]{0,2,1:T(8,128)S(1)}) fusion(f32[64,16]{0,1:T(8,128)S(1)} %convolution_multiply_fusion, bf16[16,32,4224]{2,1,0:T(8,128)(2,1)S(1)} %get-tuple-element.46, bf16[16,32,4224]{2,1,0:T(8,128)(2,1)S(1)} %get-tuple-element.45, bf16[64,4224]{1,0:T(8,128)(2,1)S(1)} %get-tuple-element.43, ...), kind=kOutput, calls=%fused_computation.73 | convolution fusion | flops 573177792 | bytes 9867520 | tf_op jit(solution)/shard_map/while/body/eval_jaxpr/dot_general | solution.py:38
  61.1 4.9 %pmax.7 = f32[64]{0:T(128)S(1)} all-reduce(f32[64]{0:T(128)S(1)} %get-tuple-element.61), channel_id=1, replica_groups=mesh['wide'=16,'shift'=2] {'shift'}, use_global_device_ids=true, to_apply=%region_1.2 | all-reduce | flops 64 | bytes 512 | tf_op jit(solution)/shard_map/pmax | solution.py:83
  66.1 0.1 fusion.32
  66.2 5.1 %psum.14 = f32[64]{0:T(128)S(1)} all-reduce(f32[64]{0:T(128)S(1)} %fusion.32), channel_id=1, replica_groups=mesh['wide'=16,'shift'=2] {'shift'}, use_global_device_ids=true, to_apply=%region_3.4 | all-reduce | flops 64 | bytes 512 | tf_op jit(solution)/shard_map/psum | solution.py:84
  71.3 0.1 convert_reduce_fusion
  71.3 0.1 fusion.31
  71.4 0.7 fusion.17
  72.1 2.4 %fusion.13 = f32[16,32,8448]{2,1,0:T(8,128)S(1)} fusion(bf16[16,32,64]{2,1,0:T(8,128)(2,1)S(1)} %bitcast.39, bf16[64,4224]{1,0:T(8,128)(2,1)S(1)} %get-tuple-element.42, bf16[64,4224]{1,0:T(8,128)(2,1)S(1)} %get-tuple-element.34), kind=kOutput, calls=%fused_computation.22 | convolution fusion | flops 555810816 | bytes 18448384 | tf_op jit(solution)/shard_map/while/body/eval_jaxpr/dot_general | solution.py:95
  74.5 0.0 copy-start.1
  74.5 4.2 %subtract_reduce_fusion = (f32[16,4224]{1,0:T(8,128)S(1)}, f32[16,4224]{1,0:T(8,128)S(1)}) fusion(f32[16,32,8448]{2,1,0:T(8,128)S(1)} %fusion.13, f32[32,4224]{1,0:T(8,128)S(1)} %get-tuple-element.57, f32[32,4224]{1,0:T(8,128)S(1)} %get-tuple-element.56), kind=kLoop, calls=%fused_computation.5 | loop fusion | flops 17166336 | bytes 18923520 | tf_op jit(solution)/shard_map/while/body/eval_jaxpr/reduce_sum | solution.py:101
  78.7 1.0 pad_maximum_fusion
  79.6 0.0 all-reduce.3.cloned.1.call-update
  79.7 0.0 copy-done.1
  79.7 0.6 dynamic-slice.1
  80.3 0.5 log_add_fusion
  80.8 89.4 %all-reduce.3.cloned.1.call-done = f32[16,12672]{1,0:T(8,128)} async-done(((f32[16,12672]{1,0:T(8,128)}), f32[16,12672]{1,0:T(8,128)}) %all-reduce.3.cloned.1.call-update) | async-done | bytes 811024
  170.2 1.7 constant_dynamic-slice_fusion
  171.9 9.3 %psum.15 = f32[1,12672]{1,0:T(1,128)} all-reduce(f32[1,12672]{1,0:T(1,128)S(1)} %constant_dynamic-slice_fusion), channel_id=1, replica_groups=mesh['wide'=16,'shift'=2] {'shift'}, use_global_device_ids=true, to_apply=%region_8.9 | all-reduce | flops 12672 | bytes 101376 | tf_op jit(solution)/shard_map/psum | solution.py:116
  (3 shorter events, 0.1 us)
Async XLA Ops:
  7.2 46.3 %copy-start = (f32[4224]{0:T(1024)S(1)}, f32[4224]{0:T(1024)}, u32[]{:S(2)}) copy-start(f32[4224]{0:T(1024)} %param.10) | copy-start | bytes 50692
  7.2 163.0 %all-reduce.3.cloned.1.call-start = ((), (), s32[]{:S(2)}) async-start(), calls=%async_computation | async-start | bytes 1622016
  74.5 5.2 %copy-start.1 = (u32[32]{0:T(128)S(1)}, u32[32]{0:T(128)}, u32[]{:S(2)}) copy-start(u32[32]{0:T(128)} %constant.75) | copy-start | bytes 388
Sparse Core Ops, SparseCore 0:
  79.8 90.3 all-reduce.2
where the time goes:
time: 188 us
  waiting for transfers between devices  89.4 us (48%)
  blocking collectives  62.5 us (33%)
  between operations  14.1 us (8%)
  other arithmetic  10.9 us (6%)
  matrix products  8.68 us (5%)
  local copies, waits for them, and re-layouts  2.31 us (1%)
    unnamed x2, waiting for transfers between devices  89.4 us
    all_gather x1, blocking collectives, local(): gathered_ctf = lax.all_gather(ctf_curves, 'wide', axis=0, tiled=True)  24.1 us
    all_gather x1, blocking collectives, local(): slab = lax.all_gather(projections, 'wide', axis=0, tiled=True)  19.1 us
    psum x1, blocking collectives, local(): insertion = lax.psum(summed, 'shift')  9.26 us
    psum x1, blocking collectives, local(): lax.psum(jnp.sum(jnp.exp(scores - row_max[:, None]), 1), 'shift')  5.1 us
    pmax x1, blocking collectives, local(): row_max = lax.pmax(local_max, 'shift')  4.93 us
    reduce_sum x1, other arithmetic, one_block(): jnp.sum(upd_real * cos_table[None] - upd_imag * sin_table[None], 1)  4.2 us
  transfers between devices with their start and end apart: 1, of which 1 were waited for; matrix products, arithmetic and copies ran while one was open for 1% of the time, Pallas kernels for 0%

commit v1 on v0

--- a/solution.py
+++ b/solution.py
@@ -70,7 +70,22 @@
     filtered = jnp.concatenate([ctf_row * real_part, ctf_row * imag_part], 1).astype(jnp.bfloat16)
     weight_sq = ctf_row * ctf_row * inv_noise[None, :]
     ctf_square = ctf_row * ctf_row
-    slab = lax.all_gather(projections, "wide", axis=0, tiled=True)
+    ways, here, step = (lax.axis_size("wide"), lax.axis_index("wide"), projections.shape[0])
+    lengths = [n * ways if d == 0 else n for d, n in enumerate(projections.shape)]
+    slab = lax.dynamic_update_slice_in_dim(
+        jnp.zeros(lengths, projections.dtype), projections, here * step, axis=0
+    )
+    going_up = going_down = projections
+    for far in range(1, ways // 2 + 1):
+        going_up = lax.ppermute(going_up, "wide", [(d, (d + 1) % ways) for d in range(ways)])
+        slab = lax.dynamic_update_slice_in_dim(slab, going_up, (here - far) % ways * step, axis=0)
+        if 2 * far < ways:
+            going_down = lax.ppermute(
+                going_down, "wide", [(d, (d - 1) % ways) for d in range(ways)]
+            )
+            slab = lax.dynamic_update_slice_in_dim(
+                slab, going_down, (here + far) % ways * step, axis=0
+            )
     amount = slab.shape[0]
     block_len = math.gcd(amount, 16)
     blocks = slab.reshape(amount // block_len, block_len, slab.shape[1])

time: 188 us -> 228 us (1.21)
  starting transfers between devices: 0.04 us -> 28.9 us
  blocking collectives: 62.5 us -> 38.4 us
  local copies, waits for them, and re-layouts: 2.31 us -> 26.1 us
  waiting for transfers between devices: 89.4 us -> 97.8 us
    ppermute x0 -> x15, starting transfers between devices: none -> 28.8 us  [the longest x7 28.3 us: local(): lax.ppermute(going_down, 'wide', [(d, (d - 1) % ways) for d in range(ways)])]
    dynamic_update_slice x0 -> x16, local copies, waits for them, and re-layouts: none -> 23.7 us  [the longest x8 12.2 us: local(): lax.dynamic_update_slice_in_dim(slab, going_up, (here - far) % ways * ste...]
    all_gather x1 -> x0, blocking collectives: 19.1 us -> none  [local(): slab = lax.all_gather(projections, 'wide', axis=0, tiled=True)]
    ppermute x0 -> x15, waiting for transfers between devices: none -> 7.5 us  [the longest x8 6.5 us: local(): lax.ppermute(going_up, 'wide', [(d, (d + 1) % ways) for d in range(ways)])]
    all_gather x1, blocking collectives: 24.1 us -> 19.1 us  [local(): gathered_ctf = lax.all_gather(ctf_curves, 'wide', axis=0, tiled=True)]
  transfers between devices with their start and end apart: 1 -> 16, of which waited for: 1 -> 9; matrix products, arithmetic and copies ran while one was open for 1% -> 13% of each run, Pallas kernels for 0% -> 0%
where the time goes in v1:
time: 228 us; the launch traced here: 227 us
  waiting for transfers between devices  97.8 us (43%)
  blocking collectives  38.4 us (17%)
  starting transfers between devices  28.9 us (13%)
  local copies, waits for them, and re-layouts  26.1 us (11%)
  between operations  14.4 us (6%)
  other arithmetic  10.9 us (5%)
  matrix products  10.4 us (5%)
    unnamed x2, waiting for transfers between devices  90.3 us
    ppermute x7, starting transfers between devices, local(): lax.ppermute(going_down, 'wide', [(d, (d - 1) % ways) for d in range(ways)])  28.3 us
    all_gather x1, blocking collectives, local(): gathered_ctf = lax.all_gather(ctf_curves, 'wide', axis=0, tiled=True)  19.1 us
    dynamic_update_slice x8, local copies, waits for them, and re-layouts, local(): lax.dynamic_update_slice_in_dim(slab, going_up, (here - far) % ways * ste...  12.2 us
    dynamic_update_slice x7, local copies, waits for them, and re-layouts, local(): lax.dynamic_update_slice_in_dim(slab, going_down, (here + far) % ways * s...  10.7 us
    psum x1, blocking collectives, local(): insertion = lax.psum(summed, 'shift')  9.26 us
    ppermute x8, waiting for transfers between devices, local(): lax.ppermute(going_up, 'wide', [(d, (d + 1) % ways) for d in range(ways)])  6.5 us
    psum x1, blocking collectives, local(): lax.psum(jnp.sum(jnp.exp(scores - row_max[:, None]), 1), 'shift')  5.14 us
  transfers between devices with their start and end apart: 16, of which 9 were waited for; matrix products, arithmetic and copies ran while one was open for 13% of the time, Pallas kernels for 0%

profile of v1, /device:TPU:0, one launch (start us, length us, event | category | flops | bytes accessed | tf_op | source)
XLA Modules:
  0.0 226.9 jit_solution(16266990487398225072)
XLA Ops:
  7.8 5.0 %collective-permute-start.1 = (bf16[1,8448]{1,0:T(2,128)(2,1)}, bf16[1,8448]{1,0:T(2,128)(2,1)S(1)}, u32[]{:S(2)}, u32[]{:S(2)}) collective-permute-start(bf16[1,8448]{1,0:T(2,128)(2,1)} %param.9), channel_id=1, source_target_pairs={{0,30},{2,0},{4,2},{6,4},{8,6},{10,8},{12,10},{14,12},{16,14},{18,... | collective-permute-start | bytes 50696 | tf_op jit(solution)/shard_map/ppermute | solution.py:83
  12.8 1.8 collective-permute-done
  14.7 4.3 %collective-permute-start.3 = (bf16[1,8448]{1,0:T(2,128)(2,1)S(1)}, bf16[1,8448]{1,0:T(2,128)(2,1)S(1)}, u32[]{:S(2)}, u32[]{:S(2)}) collective-permute-start(bf16[1,8448]{1,0:T(2,128)(2,1)S(1)} %collective-permute-done.1), channel_id=1, source_target_pairs={{0,30},{2,0},{4,2},{6,4},{8,6},{10,8},{12,10},{14,12},{16,14},{18,... | collective-permute-start | bytes 50696 | tf_op jit(solution)/shard_map/ppermute | solution.py:83
  19.1 1.5 collective-permute-done.2
  20.7 4.4 %collective-permute-start.5 = (bf16[1,8448]{1,0:T(2,128)(2,1)S(1)}, bf16[1,8448]{1,0:T(2,128)(2,1)S(1)}, u32[]{:S(2)}, u32[]{:S(2)}) collective-permute-start(bf16[1,8448]{1,0:T(2,128)(2,1)S(1)} %collective-permute-done.3), channel_id=1, source_target_pairs={{0,30},{2,0},{4,2},{6,4},{8,6},{10,8},{12,10},{14,12},{16,14},{18,... | collective-permute-start | bytes 50696 | tf_op jit(solution)/shard_map/ppermute | solution.py:83
  25.1 1.5 collective-permute-done.4
  27.4 4.5 %collective-permute-start.7 = (bf16[1,8448]{1,0:T(2,128)(2,1)S(1)}, bf16[1,8448]{1,0:T(2,128)(2,1)S(1)}, u32[]{:S(2)}, u32[]{:S(2)}) collective-permute-start(bf16[1,8448]{1,0:T(2,128)(2,1)S(1)} %collective-permute-done.5), channel_id=1, source_target_pairs={{0,30},{2,0},{4,2},{6,4},{8,6},{10,8},{12,10},{14,12},{16,14},{18,... | collective-permute-start | bytes 50696 | tf_op jit(solution)/shard_map/ppermute | solution.py:83
  33.5 4.4 %collective-permute-start.9 = (bf16[1,8448]{1,0:T(2,128)(2,1)S(1)}, bf16[1,8448]{1,0:T(2,128)(2,1)S(1)}, u32[]{:S(2)}, u32[]{:S(2)}) collective-permute-start(bf16[1,8448]{1,0:T(2,128)(2,1)S(1)} %collective-permute-done.7), channel_id=1, source_target_pairs={{0,30},{2,0},{4,2},{6,4},{8,6},{10,8},{12,10},{14,12},{16,14},{18,... | collective-permute-start | bytes 50696 | tf_op jit(solution)/shard_map/ppermute | solution.py:83
  38.9 2.0 fusion.21
  40.9 4.5 %collective-permute-start.11 = (bf16[1,8448]{1,0:T(2,128)(2,1)S(1)}, bf16[1,8448]{1,0:T(2,128)(2,1)}, u32[]{:S(2)}, u32[]{:S(2)}) collective-permute-start(bf16[1,8448]{1,0:T(2,128)(2,1)S(1)} %collective-permute-done.9), channel_id=1, source_target_pairs={{0,30},{2,0},{4,2},{6,4},{8,6},{10,8},{12,10},{14,12},{16,14},{18,... | collective-permute-start | bytes 50696 | tf_op jit(solution)/shard_map/ppermute | solution.py:83
  45.4 19.1 %all-gather = f32[16,1,4224]{2,1,0:T(1,128)S(1)} all-gather(f32[1,1,4224]{2,1,0:T(1,128)} %bitcast.34), channel_id=1, replica_groups=mesh['wide'=16,'shift'=2] {'wide'}, dimensions={0}, use_global_device_ids=true | all-gather | bytes 287232 | tf_op jit(solution)/shard_map/all_gather | solution.py:57
  65.5 3.1 %fusion.8 = (bf16[64,4224]{1,0:T(8,128)(2,1)S(1)}, bf16[64,4224]{1,0:T(8,128)(2,1)S(1)}, bf16[64,4224]{1,0:T(8,128)(2,1)}, bf16[64,4224]{1,0:T(8,128)(2,1)}, f32[64,4224]{1,0:T(8,128)S(1)}) fusion(bf16[64,8448]{1,0:T(8,128)(2,1)} %param.6, f32[4224]{0:T(1024)} %param.10, f32[16,1,4224]{2,1,0:T(1,128)S(1)} %all-gather, s32[64]{0:T(128)} %bitcast.35), kind=kOutput, calls=%fused_computation.15 | convolution fusion | flops 54879232 | bytes 4612864 | tf_op jit(solution)/shard_map/dot_general | solution.py:61
  69.6 1.5 dynamic_update_slice.87
  71.1 1.5 dynamic_update_slice.88
  72.7 1.5 dynamic_update_slice.89
  74.2 1.5 dynamic_update_slice.90
  75.7 1.5 dynamic_update_slice.91
  78.8 1.5 dynamic_update_slice.93
  80.3 1.5 dynamic_update_slice.94
  84.9 1.5 dynamic_update_slice.97
  86.4 1.5 dynamic_update_slice.98
  89.5 1.5 dynamic_update_slice.100
  92.6 1.8 convolution_multiply_fusion
  94.5 2.2 add_convert_fusion
  96.7 2.4 %fusion.46 = (f32[64]{0:T(128)S(1)}, f32[64,16,32]{0,2,1:T(8,128)S(1)}) fusion(f32[64,16]{0,1:T(8,128)S(1)} %convolution_multiply_fusion, bf16[16,32,4224]{2,1,0:T(8,128)(2,1)S(1)} %get-tuple-element.46, bf16[16,32,4224]{2,1,0:T(8,128)(2,1)S(1)} %get-tuple-element.45, bf16[64,4224]{1,0:T(8,128)(2,1)S(1)} %copy-done, bf16[64,4224]{1,0:T(8,128)(2,1)S(1)} %copy-done.1), kind=kOutput, calls=%fused_computation.72 | convolution fusion | flops 573177792 | bytes 9867520 | tf_op jit(solution)/shard_map/while/body/eval_jaxpr/dot_general | solution.py:38
  99.1 4.9 %pmax.7 = f32[64]{0:T(128)S(1)} all-reduce(f32[64]{0:T(128)S(1)} %get-tuple-element.61), channel_id=1, replica_groups=mesh['wide'=16,'shift'=2] {'shift'}, use_global_device_ids=true, to_apply=%region_1.2 | all-reduce | flops 64 | bytes 512 | tf_op jit(solution)/shard_map/pmax | solution.py:98
  104.1 5.1 %psum.14 = f32[64]{0:T(128)S(1)} all-reduce(f32[64]{0:T(128)S(1)} %fusion.32), channel_id=1, replica_groups=mesh['wide'=16,'shift'=2] {'shift'}, use_global_device_ids=true, to_apply=%region_3.4 | all-reduce | flops 64 | bytes 512 | tf_op jit(solution)/shard_map/psum | solution.py:99
  110.0 2.4 %fusion.13 = f32[16,32,8448]{2,1,0:T(8,128)S(1)} fusion(bf16[16,32,64]{2,1,0:T(8,128)(2,1)S(1)} %bitcast.33, bf16[64,4224]{1,0:T(8,128)(2,1)S(1)} %get-tuple-element.42, bf16[64,4224]{1,0:T(8,128)(2,1)S(1)} %get-tuple-element.34), kind=kOutput, calls=%fused_computation.22 | convolution fusion | flops 555810816 | bytes 18448384 | tf_op jit(solution)/shard_map/while/body/eval_jaxpr/dot_general | solution.py:110
  112.4 4.2 %subtract_reduce_fusion = (f32[16,4224]{1,0:T(8,128)S(1)}, f32[16,4224]{1,0:T(8,128)S(1)}) fusion(f32[16,32,8448]{2,1,0:T(8,128)S(1)} %fusion.13, f32[32,4224]{1,0:T(8,128)S(1)} %get-tuple-element.57, f32[32,4224]{1,0:T(8,128)S(1)} %get-tuple-element.56), kind=kLoop, calls=%fused_computation.5 | loop fusion | flops 17166336 | bytes 18923520 | tf_op jit(solution)/shard_map/while/body/eval_jaxpr/reduce_sum | solution.py:116
  118.8 90.3 %all-reduce.3.cloned.1.call-done = f32[16,12672]{1,0:T(8,128)} async-done(((f32[16,12672]{1,0:T(8,128)}), f32[16,12672]{1,0:T(8,128)}) %all-reduce.3.cloned.1.call-update) | async-done | bytes 811024
  209.1 1.7 constant_dynamic-slice_fusion
  210.8 9.3 %psum.15 = f32[1,12672]{1,0:T(1,128)} all-reduce(f32[1,12672]{1,0:T(1,128)S(1)} %constant_dynamic-slice_fusion), channel_id=1, replica_groups=mesh['wide'=16,'shift'=2] {'shift'}, use_global_device_ids=true, to_apply=%region_8.9 | all-reduce | flops 12672 | bytes 101376 | tf_op jit(solution)/shard_map/psum | solution.py:131
  (70 shorter events, 16.7 us)
Async XLA Ops:
  7.2 61.5 %copy-start.2 = (bf16[1,8448]{1,0:T(2,128)(2,1)S(1)}, bf16[1,8448]{1,0:T(2,128)(2,1)}, u32[]{:S(2)}) copy-start(bf16[1,8448]{1,0:T(2,128)(2,1)} %param.9) | copy-start | bytes 50692
  7.2 201.9 %all-reduce.3.cloned.1.call-start = ((), (), s32[]{:S(2)}) async-start(), calls=%async_computation | async-start | bytes 1622016
  7.2 7.3 %collective-permute-start = (bf16[1,8448]{1,0:T(2,128)(2,1)}, bf16[1,8448]{1,0:T(2,128)(2,1)S(1)}, u32[]{:S(2)}, u32[]{:S(2)}) collective-permute-start(bf16[1,8448]{1,0:T(2,128)(2,1)} %param.9), channel_id=1, source_target_pairs={{0,2},{2,4},{4,6},{6,8},{8,10},{10,12},{12,14},{14,16},{16,18},{18... | collective-permute-start | bytes 50696 | tf_op jit(solution)/shard_map/ppermute | solution.py:80
  7.8 7.0 %collective-permute-start.1 = (bf16[1,8448]{1,0:T(2,128)(2,1)}, bf16[1,8448]{1,0:T(2,128)(2,1)S(1)}, u32[]{:S(2)}, u32[]{:S(2)}) collective-permute-start(bf16[1,8448]{1,0:T(2,128)(2,1)} %param.9), channel_id=1, source_target_pairs={{0,30},{2,0},{4,2},{6,4},{8,6},{10,8},{12,10},{14,12},{16,14},{18,... | collective-permute-start | bytes 50696 | tf_op jit(solution)/shard_map/ppermute | solution.py:83
  14.6 24.2 %copy-start.3 = (bf16[1,8448]{1,0:T(2,128)(2,1)}, bf16[1,8448]{1,0:T(2,128)(2,1)S(1)}, u32[]{:S(2)}) copy-start(bf16[1,8448]{1,0:T(2,128)(2,1)S(1)} %collective-permute-done) | copy-start | bytes 50692
  14.6 6.0 %collective-permute-start.2 = (bf16[1,8448]{1,0:T(2,128)(2,1)S(1)}, bf16[1,8448]{1,0:T(2,128)(2,1)S(1)}, u32[]{:S(2)}, u32[]{:S(2)}) collective-permute-start(bf16[1,8448]{1,0:T(2,128)(2,1)S(1)} %collective-permute-done), channel_id=1, source_target_pairs={{0,2},{2,4},{4,6},{6,8},{8,10},{10,12},{12,14},{14,16},{16,18},{18... | collective-permute-start | bytes 50696 | tf_op jit(solution)/shard_map/ppermute | solution.py:80
  14.7 24.1 %copy-start.4 = (bf16[1,8448]{1,0:T(2,128)(2,1)}, bf16[1,8448]{1,0:T(2,128)(2,1)S(1)}, u32[]{:S(2)}) copy-start(bf16[1,8448]{1,0:T(2,128)(2,1)S(1)} %collective-permute-done.1) | copy-start | bytes 50692
  14.7 5.9 %collective-permute-start.3 = (bf16[1,8448]{1,0:T(2,128)(2,1)S(1)}, bf16[1,8448]{1,0:T(2,128)(2,1)S(1)}, u32[]{:S(2)}, u32[]{:S(2)}) collective-permute-start(bf16[1,8448]{1,0:T(2,128)(2,1)S(1)} %collective-permute-done.1), channel_id=1, source_target_pairs={{0,30},{2,0},{4,2},{6,4},{8,6},{10,8},{12,10},{14,12},{16,14},{18,... | collective-permute-start | bytes 50696 | tf_op jit(solution)/shard_map/ppermute | solution.py:83
  20.6 18.2 %copy-start.5 = (bf16[1,8448]{1,0:T(2,128)(2,1)}, bf16[1,8448]{1,0:T(2,128)(2,1)S(1)}, u32[]{:S(2)}) copy-start(bf16[1,8448]{1,0:T(2,128)(2,1)S(1)} %collective-permute-done.2) | copy-start | bytes 50692
  20.6 6.0 %collective-permute-start.4 = (bf16[1,8448]{1,0:T(2,128)(2,1)S(1)}, bf16[1,8448]{1,0:T(2,128)(2,1)S(1)}, u32[]{:S(2)}, u32[]{:S(2)}) collective-permute-start(bf16[1,8448]{1,0:T(2,128)(2,1)S(1)} %collective-permute-done.2), channel_id=1, source_target_pairs={{0,2},{2,4},{4,6},{6,8},{8,10},{10,12},{12,14},{14,16},{16,18},{18... | collective-permute-start | bytes 50696 | tf_op jit(solution)/shard_map/ppermute | solution.py:80
  20.7 18.2 %copy-start.6 = (bf16[1,8448]{1,0:T(2,128)(2,1)}, bf16[1,8448]{1,0:T(2,128)(2,1)S(1)}, u32[]{:S(2)}) copy-start(bf16[1,8448]{1,0:T(2,128)(2,1)S(1)} %collective-permute-done.3) | copy-start | bytes 50692
  20.7 6.8 %collective-permute-start.5 = (bf16[1,8448]{1,0:T(2,128)(2,1)S(1)}, bf16[1,8448]{1,0:T(2,128)(2,1)S(1)}, u32[]{:S(2)}, u32[]{:S(2)}) collective-permute-start(bf16[1,8448]{1,0:T(2,128)(2,1)S(1)} %collective-permute-done.3), channel_id=1, source_target_pairs={{0,30},{2,0},{4,2},{6,4},{8,6},{10,8},{12,10},{14,12},{16,14},{18,... | collective-permute-start | bytes 50696 | tf_op jit(solution)/shard_map/ppermute | solution.py:83
  26.7 12.2 %copy-start.7 = (bf16[1,8448]{1,0:T(2,128)(2,1)}, bf16[1,8448]{1,0:T(2,128)(2,1)S(1)}, u32[]{:S(2)}) copy-start(bf16[1,8448]{1,0:T(2,128)(2,1)S(1)} %collective-permute-done.4) | copy-start | bytes 50692
  26.7 6.1 %collective-permute-start.6 = (bf16[1,8448]{1,0:T(2,128)(2,1)S(1)}, bf16[1,8448]{1,0:T(2,128)(2,1)S(1)}, u32[]{:S(2)}, u32[]{:S(2)}) collective-permute-start(bf16[1,8448]{1,0:T(2,128)(2,1)S(1)} %collective-permute-done.4), channel_id=1, source_target_pairs={{0,2},{2,4},{4,6},{6,8},{8,10},{10,12},{12,14},{14,16},{16,18},{18... | collective-permute-start | bytes 50696 | tf_op jit(solution)/shard_map/ppermute | solution.py:80
  27.4 11.4 %copy-start.8 = (bf16[1,8448]{1,0:T(2,128)(2,1)}, bf16[1,8448]{1,0:T(2,128)(2,1)S(1)}, u32[]{:S(2)}) copy-start(bf16[1,8448]{1,0:T(2,128)(2,1)S(1)} %collective-permute-done.5) | copy-start | bytes 50692
  27.4 6.1 %collective-permute-start.7 = (bf16[1,8448]{1,0:T(2,128)(2,1)S(1)}, bf16[1,8448]{1,0:T(2,128)(2,1)S(1)}, u32[]{:S(2)}, u32[]{:S(2)}) collective-permute-start(bf16[1,8448]{1,0:T(2,128)(2,1)S(1)} %collective-permute-done.5), channel_id=1, source_target_pairs={{0,30},{2,0},{4,2},{6,4},{8,6},{10,8},{12,10},{14,12},{16,14},{18,... | collective-permute-start | bytes 50696 | tf_op jit(solution)/shard_map/ppermute | solution.py:83
  32.8 6.1 %copy-start.9 = (bf16[1,8448]{1,0:T(2,128)(2,1)}, bf16[1,8448]{1,0:T(2,128)(2,1)S(1)}, u32[]{:S(2)}) copy-start(bf16[1,8448]{1,0:T(2,128)(2,1)S(1)} %collective-permute-done.6) | copy-start | bytes 50692
  32.8 6.0 %collective-permute-start.8 = (bf16[1,8448]{1,0:T(2,128)(2,1)S(1)}, bf16[1,8448]{1,0:T(2,128)(2,1)S(1)}, u32[]{:S(2)}, u32[]{:S(2)}) collective-permute-start(bf16[1,8448]{1,0:T(2,128)(2,1)S(1)} %collective-permute-done.6), channel_id=1, source_target_pairs={{0,2},{2,4},{4,6},{6,8},{8,10},{10,12},{12,14},{14,16},{16,18},{18... | collective-permute-start | bytes 50696 | tf_op jit(solution)/shard_map/ppermute | solution.py:80
  33.5 32.0 %copy-start.10 = (bf16[1,8448]{1,0:T(2,128)(2,1)}, bf16[1,8448]{1,0:T(2,128)(2,1)S(1)}, u32[]{:S(2)}) copy-start(bf16[1,8448]{1,0:T(2,128)(2,1)S(1)} %collective-permute-done.7) | copy-start | bytes 50692
  33.5 7.3 %collective-permute-start.9 = (bf16[1,8448]{1,0:T(2,128)(2,1)S(1)}, bf16[1,8448]{1,0:T(2,128)(2,1)S(1)}, u32[]{:S(2)}, u32[]{:S(2)}) collective-permute-start(bf16[1,8448]{1,0:T(2,128)(2,1)S(1)} %collective-permute-done.7), channel_id=1, source_target_pairs={{0,30},{2,0},{4,2},{6,4},{8,6},{10,8},{12,10},{14,12},{16,14},{18,... | collective-permute-start | bytes 50696 | tf_op jit(solution)/shard_map/ppermute | solution.py:83
  38.8 26.7 %copy-start.11 = (bf16[1,8448]{1,0:T(2,128)(2,1)}, bf16[1,8448]{1,0:T(2,128)(2,1)S(1)}, u32[]{:S(2)}) copy-start(bf16[1,8448]{1,0:T(2,128)(2,1)S(1)} %collective-permute-done.8) | copy-start | bytes 50692
  38.8 6.6 %collective-permute-start.10 = (bf16[1,8448]{1,0:T(2,128)(2,1)S(1)}, bf16[1,8448]{1,0:T(2,128)(2,1)S(1)}, u32[]{:S(2)}, u32[]{:S(2)}) collective-permute-start(bf16[1,8448]{1,0:T(2,128)(2,1)S(1)} %collective-permute-done.8), channel_id=1, source_target_pairs={{0,2},{2,4},{4,6},{6,8},{8,10},{10,12},{12,14},{14,16},{16,18},{18... | collective-permute-start | bytes 50696 | tf_op jit(solution)/shard_map/ppermute | solution.py:80
  40.9 24.6 %copy-start.12 = (bf16[1,8448]{1,0:T(2,128)(2,1)}, bf16[1,8448]{1,0:T(2,128)(2,1)S(1)}, u32[]{:S(2)}) copy-start(bf16[1,8448]{1,0:T(2,128)(2,1)S(1)} %collective-permute-done.9) | copy-start | bytes 50692
  40.9 23.5 %collective-permute-start.11 = (bf16[1,8448]{1,0:T(2,128)(2,1)S(1)}, bf16[1,8448]{1,0:T(2,128)(2,1)}, u32[]{:S(2)}, u32[]{:S(2)}) collective-permute-start(bf16[1,8448]{1,0:T(2,128)(2,1)S(1)} %collective-permute-done.9), channel_id=1, source_target_pairs={{0,30},{2,0},{4,2},{6,4},{8,6},{10,8},{12,10},{14,12},{16,14},{18,... | collective-permute-start | bytes 50696 | tf_op jit(solution)/shard_map/ppermute | solution.py:83
  45.4 20.2 %copy-start.13 = (bf16[1,8448]{1,0:T(2,128)(2,1)}, bf16[1,8448]{1,0:T(2,128)(2,1)S(1)}, u32[]{:S(2)}) copy-start(bf16[1,8448]{1,0:T(2,128)(2,1)S(1)} %collective-permute-done.10) | copy-start | bytes 50692
  45.4 20.1 %collective-permute-start.12 = (bf16[1,8448]{1,0:T(2,128)(2,1)S(1)}, bf16[1,8448]{1,0:T(2,128)(2,1)}, u32[]{:S(2)}, u32[]{:S(2)}) collective-permute-start(bf16[1,8448]{1,0:T(2,128)(2,1)S(1)} %collective-permute-done.10), channel_id=1, source_target_pairs={{0,2},{2,4},{4,6},{6,8},{8,10},{10,12},{12,14},{14,16},{16,18},{18... | collective-permute-start | bytes 50696 | tf_op jit(solution)/shard_map/ppermute | solution.py:80
  64.4 25.1 %collective-permute-start.13 = (bf16[1,8448]{1,0:T(2,128)(2,1)}, bf16[1,8448]{1,0:T(2,128)(2,1)}, u32[]{:S(2)}, u32[]{:S(2)}) collective-permute-start(bf16[1,8448]{1,0:T(2,128)(2,1)} %collective-permute-done.11), channel_id=1, source_target_pairs={{0,30},{2,0},{4,2},{6,4},{8,6},{10,8},{12,10},{14,12},{16,14},{18,... | collective-permute-start | bytes 50696 | tf_op jit(solution)/shard_map/ppermute | solution.py:83
  65.5 25.6 %collective-permute-start.14 = (bf16[1,8448]{1,0:T(2,128)(2,1)}, bf16[1,8448]{1,0:T(2,128)(2,1)}, u32[]{:S(2)}, u32[]{:S(2)}) collective-permute-start(bf16[1,8448]{1,0:T(2,128)(2,1)} %collective-permute-done.12), channel_id=1, source_target_pairs={{0,2},{2,4},{4,6},{6,8},{8,10},{10,12},{12,14},{14,16},{16,18},{18... | collective-permute-start | bytes 50696 | tf_op jit(solution)/shard_map/ppermute | solution.py:80
  94.5 2.2 copy-start
  94.5 2.2 copy-start.1
  112.4 5.2 %copy-start.14 = (u32[32]{0:T(128)S(1)}, u32[32]{0:T(128)}, u32[]{:S(2)}) copy-start(u32[32]{0:T(128)} %constant.211) | copy-start | bytes 388
Sparse Core Ops, SparseCore 0:
  117.8 91.2 all-reduce.2
